TPU v7x, 32 devices: a whole 2x2x4 slice. The times are simulated.
32 devices in a mesh: aux: 4 (over z), pair: 8 (over y, x, core).
Axes of the slice: x: 2, y: 2, z: 4, core: 2. Of those that a mesh axis runs over, the one named last changes fastest.
Arguments:
- b_three: bfloat16 [4096, 2048], P('pair', 'aux'), may hold values from -0.13183594 to 0.13183594
- metric: bfloat16 [2048, 2048], P(None, 'aux'), may hold values from -1 to 2
- aux_map: int32 [64, 32], P('pair', 'aux'), may hold values 0 or 1
- domains: int32 [80, 4], replicated, may hold values from 0 to 63, as said below
- counts: int32 [80], P('pair'), may hold values from 1 to 4, as said below
Outputs:
- pair_integrals: float32 [80, 256, 256], P('pair', 'aux')
Inputs may be any that keep to these rules, and one draw needn't show every extreme that they name: `domains`: of the 40 slots of the pairs of one index of pair (pairs q * 10 to (q + 1) * 10 - 1), at most 5 name blocks held by one index of pair (blocks o * 8 to (o + 1) * 8 - 1), and exactly 5 for some such index in every draw. `counts`: slots at or past a pair's count are padding.
All inputs are finite; a program needn't handle non-finite values. No bound on the sum of `aux_map` on one device may be relied on, other than what follows from the above.
Results may differ from a plain program's by a relative error of at most 0.00079.
Values may be sent and summed in bfloat16 or wider, within the bound.
A program may use at most 64 MiB of HBM per device.

v0:
```python
import jax
import jax.numpy as jnp
from jax import lax
from jax.sharding import PartitionSpec as P


def per_device(b_three, metric, aux_map, domains, counts):
    rows_dev, aux_dev = b_three.shape
    blocks_dev, aux_blocks = aux_map.shape
    width_cw = rows_dev // blocks_dev
    aux_width = aux_dev // aux_blocks
    keep_mask = aux_map.astype(jnp.bfloat16)
    masked = (
        b_three.reshape(blocks_dev, width_cw, aux_blocks, aux_width) * keep_mask[:, None, :, None]
    ).reshape(rows_dev, aux_dev)
    fitted = jnp.dot(
        lax.all_gather(masked, "aux", axis=1, tiled=True),
        metric,
        preferred_element_type=jnp.float32,
    ).astype(jnp.bfloat16)
    block_table = fitted.reshape(blocks_dev, width_cw * aux_dev)
    peer_count = lax.axis_size("pair")
    own_index = lax.axis_index("pair")
    pairs_dev = counts.shape[0]
    domain_max = domains.shape[1]
    slot_count = pairs_dev * domain_max
    all_domains = domains.reshape(peer_count, slot_count)
    own_domains = lax.dynamic_slice_in_dim(all_domains, own_index, 1, 0)[0]
    shard_piece = lax.all_gather(block_table, "pair", axis=0, tiled=True)
    block_ids = jnp.arange(shard_piece.shape[0], dtype=jnp.int32)
    onehot = (own_domains[:, None] == block_ids[None, :]).astype(jnp.bfloat16)
    chosen = jnp.dot(onehot, shard_piece, preferred_element_type=jnp.float32).astype(jnp.bfloat16)
    stacks = chosen.reshape(pairs_dev, domain_max * width_cw, aux_dev)
    partial_value = jnp.einsum("pax,pbx->pab", stacks, stacks, preferred_element_type=jnp.float32)
    slot_of = jnp.arange(domain_max * width_cw, dtype=jnp.int32) // width_cw
    live_rows = slot_of[None, :] < counts[:, None]
    partial_value = jnp.where(
        live_rows[:, :, None] & live_rows[:, None, :], partial_value, jnp.zeros_like(partial_value)
    )
    return lax.psum_scatter(partial_value, "aux", scatter_dimension=1, tiled=True)


def solution(mesh):
    return jax.shard_map(
        per_device,
        mesh=mesh,
        in_specs=(P("pair", "aux"), P(None, "aux"), P("pair", "aux"), P(), P("pair")),
        out_specs=P("pair", "aux", None),
        check_vma=False,
    )
```

profile of v0, /device:TPU:0, one launch (start us, length us, event | category | flops | bytes accessed | tf_op | source)
XLA Modules:
  0.0 172.9 jit_solution(9193353961309677917)
XLA Ops:
  6.5 0.0 copy-start
  6.5 0.0 all-gather.3.cloned.1.call-start
  6.5 0.8 convert_element_type.10
  7.4 0.2 mul.11
  7.6 1.4 mul.12
  9.0 2.1 %mul.13 = bf16[512,512]{1,0:T(8,128)(2,1)} multiply(bf16[512,512]{1,0:T(8,128)(2,1)} %param.5, bf16[512,512]{1,0:T(8,128)(2,1)} %mul.12) | non-fusion elementwise | flops 262144 | bytes 1572864 | tf_op jit(solution)/shard_map/mul | solution.py:14
  11.1 0.0 all-gather.3.cloned.1.call-update
  11.1 0.0 copy-start.1
  11.2 0.0 copy-start.2
  11.2 0.0 all-gather.5.cloned.1.call-start
  11.2 48.5 %all-gather.3.cloned.1.call-done = bf16[512,2048]{1,0:T(8,128)(2,1)} async-done(((bf16[512,512]{1,0:T(8,128)(2,1)}), bf16[512,2048]{1,0:T(8,128)(2,1)}) %all-gather.3.cloned.1.call-update) | async-done | bytes 2097168 | tf_op jit(solution)/shard_map/all_gather | solution.py:17
  59.7 2.8 %convolution_convert_fusion.1 = bf16[512,512]{1,0:T(8,128)(2,1)S(1)} fusion(bf16[512,2048]{1,0:T(8,128)(2,1)} %all-gather.3.cloned.1.call-done, bf16[2048,512]{1,0:T(8,128)(2,1)S(1)} %copy-done), kind=kOutput, calls=%fused_computation.2 | convolution fusion | flops 1074003968 | bytes 4718592 | tf_op jit(solution)/shard_map/dot_general | solution.py:16
  62.5 1.0 reshape.77
  63.6 0.0 all-gather.5.cloned.1.call-update
  63.6 0.0 reduce-scatter.2.cloned.1.call-start
  63.6 0.1 copy.6
  63.7 0.1 reshape.76
  63.9 0.1 broadcast_compare_fusion
  63.9 35.2 %all-gather.5.cloned.1.call-done = bf16[64,32768]{1,0:T(8,128)(2,1)} async-done(((bf16[8,32768]{1,0:T(8,128)(2,1)}), bf16[64,32768]{1,0:T(8,128)(2,1)}) %all-gather.5.cloned.1.call-update) | async-done | bytes 4194320 | tf_op jit(solution)/shard_map/all_gather | solution.py:29
  99.1 4.6 %convolution_convert_fusion = bf16[40,32768]{1,0:T(8,128)(2,1)} fusion(bf16[64,32768]{1,0:T(8,128)(2,1)} %all-gather.5.cloned.1.call-done, s32[40]{0:T(128)S(1)} %dynamic-slice_bitcast_fusion), kind=kOutput, calls=%fused_computation | convolution fusion | flops 169085440 | bytes 6815904 | tf_op jit(solution)/shard_map/dot_general | solution.py:32
  103.7 5.3 %reshape.78 = bf16[10,256,512]{2,1,0:T(8,128)(2,1)} reshape(bf16[40,32768]{1,0:T(8,128)(2,1)} %convolution_convert_fusion) | data formatting | bytes 5242880 | tf_op jit(solution)/shard_map/reshape | solution.py:33
  109.0 5.0 %and_select_fusion = f32[10,256,256]{2,1,0:T(8,128)} fusion(bf16[10,256,512]{2,1,0:T(8,128)(2,1)} %reshape.78, pred[10,256]{1,0:T(8,128)(4,1)S(1)} %broadcast_compare_fusion), kind=kOutput, calls=%fused_computation.1 | convolution fusion | flops 672399360 | bytes 5245440 | tf_op jit(solution)/shard_map/pax,pbx->pab/dot_general | solution.py:34
  114.0 0.0 reduce-scatter.2.cloned.1.call-update
  114.0 52.4 %reduce-scatter.2.cloned.1.call-done = f32[10,64,256]{2,1,0:T(8,128)} async-done(((f32[10,256,256]{2,1,0:T(8,128)}), f32[10,64,256]{2,1,0:T(8,128)}) %reduce-scatter.2.cloned.1.call-update) | async-done | bytes 655376 | tf_op jit(solution)/shard_map/reduce_scatter | solution.py:40
  (5 shorter events, 0.0 us)
Async XLA Ops:
  6.5 53.1 %copy-start = (bf16[2048,512]{1,0:T(8,128)(2,1)S(1)}, bf16[2048,512]{1,0:T(8,128)(2,1)}, u32[]{:S(2)}) copy-start(bf16[2048,512]{1,0:T(8,128)(2,1)} %param.6) | copy-start | bytes 6291460
  6.5 53.1 %all-gather.3.cloned.1.call-start = ((), (), s32[]{:S(2)}) async-start(), calls=%async_computation.1 | async-start | bytes 2621440 | tf_op jit(solution)/shard_map/all_gather | solution.py:17
  11.1 52.5 %copy-start.1 = (s32[80,4]{0,1:T(4,128)S(1)}, s32[80,4]{0,1:T(4,128)}, u32[]{:S(2)}) copy-start(s32[80,4]{0,1:T(4,128)} %param.8) | copy-start | bytes 3844
  11.2 52.7 %copy-start.2 = (s32[10]{0:T(128)S(1)}, s32[10]{0:T(128)}, u32[]{:S(2)}) copy-start(s32[10]{0:T(128)} %param.9) | copy-start | bytes 124
  11.2 88.0 %all-gather.5.cloned.1.call-start = ((), (), s32[]{:S(2)}) async-start(), calls=%async_computation.2 | async-start | bytes 4718592 | tf_op jit(solution)/shard_map/all_gather | solution.py:29
  63.6 102.8 %reduce-scatter.2.cloned.1.call-start = ((), (), s32[]{:S(2)}) async-start(), calls=%async_computation.3 | async-start | bytes 3276800 | tf_op jit(solution)/shard_map/reduce_scatter | solution.py:40
Sparse Core Ops, SparseCore 0:
  11.3 48.3 all-gather.2
  63.7 35.3 all-gather.4
  114.1 52.2 reduce-scatter.1
where the time goes:
time: 173 us
  waiting for transfers between devices  136 us (79%)
  between operations  13.2 us (8%)
  matrix products  12.4 us (7%)
  local copies, waits for them, and re-layouts  8.12 us (5%)
  other arithmetic  3.04 us (2%)
    reduce_scatter x1, waiting for transfers between devices, per_device(): lax.psum_scatter(partial_value, 'aux', scatter_dimension=1, tiled=True)  52.4 us
    all_gather x1, waiting for transfers between devices, per_device(): lax.all_gather(masked, 'aux', axis=1, tiled=True)  48.5 us
    all_gather x1, waiting for transfers between devices, per_device(): shard_piece = lax.all_gather(block_table, 'pair', axis=0, tiled=True)  35.2 us
    reshape x1, local copies, waits for them, and re-layouts, per_device(): stacks = chosen.reshape(pairs_dev, domain_max * width_cw, aux_dev)  5.27 us
    dot_general x1, matrix products, per_device(): jnp.einsum('pax,pbx->pab', stacks, stacks, preferred_element_type=jnp.flo...  4.97 us
    dot_general x1, matrix products, per_device(): jnp.dot(onehot, shard_piece, preferred_element_type=jnp.float32)  4.62 us
  transfers between devices with their start and end apart: 3, of which 3 were waited for; matrix products, arithmetic and copies ran while one was open for 0% of the time, Pallas kernels for 0%

commit v1 on v0

--- a/solution.py
+++ b/solution.py
@@ -2,6 +2,17 @@
 import jax.numpy as jnp
 from jax import lax
 from jax.sharding import PartitionSpec as P
+
+
+def ring_gather(x, axis, dim):
+    ways = lax.axis_size(axis)
+    pieces = [x]
+    for far in range(1, ways):
+        pieces.append(
+            lax.ppermute(pieces[far - 1], axis, [(d, (d - 1) % ways) for d in range(ways)])
+        )
+    line = jnp.concatenate(pieces, axis=dim)
+    return jnp.roll(line, lax.axis_index(axis) * x.shape[dim], axis=dim)
 
 
 def per_device(b_three, metric, aux_map, domains, counts):
@@ -14,9 +25,7 @@
         b_three.reshape(blocks_dev, width_cw, aux_blocks, aux_width) * keep_mask[:, None, :, None]
     ).reshape(rows_dev, aux_dev)
     fitted = jnp.dot(
-        lax.all_gather(masked, "aux", axis=1, tiled=True),
-        metric,
-        preferred_element_type=jnp.float32,
+        ring_gather(masked, "aux", 1), metric, preferred_element_type=jnp.float32
     ).astype(jnp.bfloat16)
     block_table = fitted.reshape(blocks_dev, width_cw * aux_dev)
     peer_count = lax.axis_size("pair")

time: 173 us -> 181 us (1.046)
  waiting for transfers between devices: 136 us -> 120 us
  starting transfers between devices: 0.09 us -> 13.7 us
  local copies, waits for them, and re-layouts: 8.12 us -> 17.4 us
    all_gather x1 -> x0, waiting for transfers between devices: 48.5 us -> none  [per_device(): lax.all_gather(masked, 'aux', axis=1, tiled=True)]
    ppermute x0 -> x3, waiting for transfers between devices: none -> 29.2 us  [ring_gather(): lax.ppermute(pieces[far - 1], axis, [(d, (d - 1) % ways) for d in range(w...]
    ppermute x0 -> x3, starting transfers between devices: none -> 13.6 us  [ring_gather(): lax.ppermute(pieces[far - 1], axis, [(d, (d - 1) % ways) for d in range(w...]
    unnamed x7 -> x15, local copies, waits for them, and re-layouts: 0.12 us -> 7.55 us
    all_gather x1, waiting for transfers between devices: 35.2 us -> 38.4 us  [per_device(): shard_piece = lax.all_gather(block_table, 'pair', axis=0, tiled=True)]
    unnamed x0 -> x1, other arithmetic: none -> 2.21 us
    mul x1 -> x0, other arithmetic: 2.12 us -> none  [per_device(): b_three.reshape(blocks_dev, width_cw, aux_blocks, aux_width)]
    concatenate x0 -> x1, local copies, waits for them, and re-layouts: none -> 1.91 us  [ring_gather(): return jnp.roll(line, lax.axis_index(axis) * x.shape[dim], axis=dim)]
  transfers between devices with their start and end apart: 3 -> 5, of which waited for: 3 -> 5; matrix products, arithmetic and copies ran while one was open for 0% -> 1% of each run, Pallas kernels for 0% -> 0%
where the time goes in v1:
time: 181 us; the launch traced here: 180 us
  waiting for transfers between devices  120 us (66%)
  local copies, waits for them, and re-layouts  17.4 us (10%)
  starting transfers between devices  13.7 us (8%)
  between operations  13.5 us (7%)
  matrix products  12.5 us (7%)
  other arithmetic  3.12 us (2%)
    reduce_scatter x1, waiting for transfers between devices, per_device(): lax.psum_scatter(partial_value, 'aux', scatter_dimension=1, tiled=True)  52.4 us
    all_gather x1, waiting for transfers between devices, per_device(): shard_piece = lax.all_gather(block_table, 'pair', axis=0, tiled=True)  38.4 us
    ppermute x3, waiting for transfers between devices, ring_gather(): lax.ppermute(pieces[far - 1], axis, [(d, (d - 1) % ways) for d in range(w...  29.2 us
    ppermute x3, starting transfers between devices, ring_gather(): lax.ppermute(pieces[far - 1], axis, [(d, (d - 1) % ways) for d in range(w...  13.6 us
    unnamed x15, local copies, waits for them, and re-layouts  7.55 us
    reshape x1, local copies, waits for them, and re-layouts, per_device(): stacks = chosen.reshape(pairs_dev, domain_max * width_cw, aux_dev)  5.25 us
    dot_general x1, matrix products, per_device(): jnp.einsum('pax,pbx->pab', stacks, stacks, preferred_element_type=jnp.flo...  4.97 us
    dot_general x1, matrix products, per_device(): jnp.dot(onehot, shard_piece, preferred_element_type=jnp.float32)  4.62 us
  transfers between devices with their start and end apart: 5, of which 5 were waited for; matrix products, arithmetic and copies ran while one was open for 1% of the time, Pallas kernels for 0%

profile of v1, /device:TPU:0, one launch (start us, length us, event | category | flops | bytes accessed | tf_op | source)
XLA Modules:
  0.0 180.2 jit_solution(1801180953366673909)
XLA Ops:
  6.5 0.8 convert_element_type.10
  7.4 0.2 mul.14
  7.6 1.4 mul.15
  9.0 2.2 %constant_dynamic-update-slice_fusion.7 = (bf16[512,4096]{1,0:T(8,128)(2,1)}, bf16[512,512]{1,0:T(8,128)(2,1)S(1)}) fusion(bf16[512,512]{1,0:T(8,128)(2,1)} %param.5, bf16[512,512]{1,0:T(8,128)(2,1)} %mul.15), kind=kLoop, calls=%fused_computation.13 | loop fusion | flops 1048575 | bytes 2097152
  11.2 5.1 %collective-permute-start = (bf16[512,512]{1,0:T(8,128)(2,1)S(1)}, bf16[512,512]{1,0:T(8,128)(2,1)S(1)}, u32[]{:S(2)}, u32[]{:S(2)}) collective-permute-start(bf16[512,512]{1,0:T(8,128)(2,1)S(1)} %get-tuple-element.6), channel_id=1, source_target_pairs={{0,24},{8,0},{16,8},{24,16},{1,25},{9,1},{17,9},{25,17},{2,26},{10... | collective-permute-start | bytes 1572872 | tf_op jit(solution)/shard_map/ppermute | solution.py:12
  16.3 11.2 %collective-permute-done = bf16[512,512]{1,0:T(8,128)(2,1)S(1)} collective-permute-done((bf16[512,512]{1,0:T(8,128)(2,1)S(1)}, bf16[512,512]{1,0:T(8,128)(2,1)S(1)}, u32[]{:S(2)}, u32[]{:S(2)}) %collective-permute-start) | collective-permute-done | bytes 524320 | tf_op jit(solution)/shard_map/ppermute | solution.py:12
  27.5 4.3 %collective-permute-start.1 = (bf16[512,512]{1,0:T(8,128)(2,1)S(1)}, bf16[512,512]{1,0:T(8,128)(2,1)S(1)}, u32[]{:S(2)}, u32[]{:S(2)}) collective-permute-start(bf16[512,512]{1,0:T(8,128)(2,1)S(1)} %collective-permute-done), channel_id=1, source_target_pairs={{0,24},{8,0},{16,8},{24,16},{1,25},{9,1},{17,9},{25,17},{2,26},{10... | collective-permute-start | bytes 1572872 | tf_op jit(solution)/shard_map/ppermute | solution.py:12
  31.7 10.3 %collective-permute-done.1 = bf16[512,512]{1,0:T(8,128)(2,1)S(1)} collective-permute-done((bf16[512,512]{1,0:T(8,128)(2,1)S(1)}, bf16[512,512]{1,0:T(8,128)(2,1)S(1)}, u32[]{:S(2)}, u32[]{:S(2)}) %collective-permute-start.1) | collective-permute-done | bytes 524320 | tf_op jit(solution)/shard_map/ppermute | solution.py:12
  42.1 4.3 %collective-permute-start.2 = (bf16[512,512]{1,0:T(8,128)(2,1)S(1)}, bf16[512,512]{1,0:T(8,128)(2,1)}, u32[]{:S(2)}, u32[]{:S(2)}) collective-permute-start(bf16[512,512]{1,0:T(8,128)(2,1)S(1)} %collective-permute-done.1), channel_id=1, source_target_pairs={{0,24},{8,0},{16,8},{24,16},{1,25},{9,1},{17,9},{25,17},{2,26},{10... | collective-permute-start | bytes 1572872 | tf_op jit(solution)/shard_map/ppermute | solution.py:12
  46.4 0.9 constant_dynamic-update-slice_fusion.6
  47.2 0.9 constant_dynamic-update-slice_fusion.5
  48.1 7.7 %collective-permute-done.2 = bf16[512,512]{1,0:T(8,128)(2,1)} collective-permute-done((bf16[512,512]{1,0:T(8,128)(2,1)S(1)}, bf16[512,512]{1,0:T(8,128)(2,1)}, u32[]{:S(2)}, u32[]{:S(2)}) %collective-permute-start.2) | collective-permute-done | bytes 524320 | tf_op jit(solution)/shard_map/ppermute | solution.py:12
  55.8 2.0 %constant_dynamic-update-slice_fusion.4 = bf16[512,4096]{1,0:T(8,128)(2,1)} fusion(bf16[512,4096]{1,0:T(8,128)(2,1)} %constant_dynamic-update-slice_fusion.5, bf16[512,512]{1,0:T(8,128)(2,1)} %collective-permute-done.2), kind=kLoop, calls=%fused_computation.10 | loop fusion | bytes 1048576
  57.8 2.0 %constant_dynamic-update-slice_fusion.3 = bf16[512,4096]{1,0:T(8,128)(2,1)} fusion(bf16[512,4096]{1,0:T(8,128)(2,1)} %constant_dynamic-update-slice_fusion.4, bf16[512,512]{1,0:T(8,128)(2,1)} %copy-done.1), kind=kLoop, calls=%fused_computation.9 | loop fusion | bytes 1048576
  59.8 0.9 constant_dynamic-update-slice_fusion.2
  60.6 0.9 constant_dynamic-update-slice_fusion.1
  61.5 1.9 %constant_dynamic-update-slice_fusion = bf16[512,4096]{1,0:T(8,128)(2,1)} fusion(bf16[512,4096]{1,0:T(8,128)(2,1)} %constant_dynamic-update-slice_fusion.1, bf16[512,512]{1,0:T(8,128)(2,1)} %collective-permute-done.2), kind=kLoop, calls=%fused_computation.6 | loop fusion | bytes 1048576 | tf_op jit(solution)/shard_map/jit(_roll_dynamic)/concatenate | solution.py:15
  63.4 2.9 %fusion.2 = bf16[512,512]{1,0:T(8,128)(2,1)S(1)} fusion(bf16[2048,512]{1,0:T(8,128)(2,1)S(1)} %copy-done, bf16[512,4096]{1,0:T(8,128)(2,1)} %constant_dynamic-update-slice_fusion, s32[]{:T(128)S(6)} %select_n.32), kind=kOutput, calls=%fused_computation.4 | convolution fusion | flops 1074003968 | bytes 4718596 | tf_op jit(solution)/shard_map/dot_general | solution.py:27
  66.3 1.0 reshape.77
  67.7 38.4 %all-gather.2.cloned.1.call-done = bf16[64,32768]{1,0:T(8,128)(2,1)} async-done(((bf16[8,32768]{1,0:T(8,128)(2,1)}), bf16[64,32768]{1,0:T(8,128)(2,1)}) %all-gather.2.cloned.1.call-update) | async-done | bytes 4194320 | tf_op jit(solution)/shard_map/all_gather | solution.py:38
  106.1 4.6 %convolution_convert_fusion = bf16[40,32768]{1,0:T(8,128)(2,1)} fusion(bf16[64,32768]{1,0:T(8,128)(2,1)} %all-gather.2.cloned.1.call-done, s32[40]{0:T(128)S(1)} %dynamic-slice_bitcast_fusion), kind=kOutput, calls=%fused_computation | convolution fusion | flops 169085440 | bytes 6815904 | tf_op jit(solution)/shard_map/dot_general | solution.py:41
  110.7 5.3 %reshape.78 = bf16[10,256,512]{2,1,0:T(8,128)(2,1)} reshape(bf16[40,32768]{1,0:T(8,128)(2,1)} %convolution_convert_fusion) | data formatting | bytes 5242880 | tf_op jit(solution)/shard_map/reshape | solution.py:42
  116.0 5.0 %and_select_fusion = f32[10,256,256]{2,1,0:T(8,128)} fusion(bf16[10,256,512]{2,1,0:T(8,128)(2,1)} %reshape.78, pred[10,256]{1,0:T(8,128)(4,1)S(1)} %broadcast_compare_fusion), kind=kOutput, calls=%fused_computation.1 | convolution fusion | flops 672399360 | bytes 5245440 | tf_op jit(solution)/shard_map/pax,pbx->pab/dot_general | solution.py:43
  121.0 52.4 %reduce-scatter.2.cloned.1.call-done = f32[10,64,256]{2,1,0:T(8,128)} async-done(((f32[10,256,256]{2,1,0:T(8,128)}), f32[10,64,256]{2,1,0:T(8,128)}) %reduce-scatter.2.cloned.1.call-update) | async-done | bytes 655376 | tf_op jit(solution)/shard_map/reduce_scatter | solution.py:49
  (17 shorter events, 0.4 us)
Async XLA Ops:
  6.5 56.9 %copy-start = (bf16[2048,512]{1,0:T(8,128)(2,1)S(1)}, bf16[2048,512]{1,0:T(8,128)(2,1)}, u32[]{:S(2)}) copy-start(bf16[2048,512]{1,0:T(8,128)(2,1)} %param.6) | copy-start | bytes 6291460
  6.5 99.6 %all-gather.2.cloned.1.call-start = ((), (), s32[]{:S(2)}) async-start(), calls=%async_computation.1 | async-start | bytes 4718592 | tf_op jit(solution)/shard_map/all_gather | solution.py:38
  11.2 30.9 %copy-start.1 = (bf16[512,512]{1,0:T(8,128)(2,1)}, bf16[512,512]{1,0:T(8,128)(2,1)S(1)}, u32[]{:S(2)}) copy-start(bf16[512,512]{1,0:T(8,128)(2,1)S(1)} %get-tuple-element.6) | copy-start | bytes 1572868
  11.2 16.3 %collective-permute-start = (bf16[512,512]{1,0:T(8,128)(2,1)S(1)}, bf16[512,512]{1,0:T(8,128)(2,1)S(1)}, u32[]{:S(2)}, u32[]{:S(2)}) collective-permute-start(bf16[512,512]{1,0:T(8,128)(2,1)S(1)} %get-tuple-element.6), channel_id=1, source_target_pairs={{0,24},{8,0},{16,8},{24,16},{1,25},{9,1},{17,9},{25,17},{2,26},{10... | collective-permute-start | bytes 1572872 | tf_op jit(solution)/shard_map/ppermute | solution.py:12
  27.5 14.6 %collective-permute-start.1 = (bf16[512,512]{1,0:T(8,128)(2,1)S(1)}, bf16[512,512]{1,0:T(8,128)(2,1)S(1)}, u32[]{:S(2)}, u32[]{:S(2)}) collective-permute-start(bf16[512,512]{1,0:T(8,128)(2,1)S(1)} %collective-permute-done), channel_id=1, source_target_pairs={{0,24},{8,0},{16,8},{24,16},{1,25},{9,1},{17,9},{25,17},{2,26},{10... | collective-permute-start | bytes 1572872 | tf_op jit(solution)/shard_map/ppermute | solution.py:12
  42.1 13.8 %collective-permute-start.2 = (bf16[512,512]{1,0:T(8,128)(2,1)S(1)}, bf16[512,512]{1,0:T(8,128)(2,1)}, u32[]{:S(2)}, u32[]{:S(2)}) collective-permute-start(bf16[512,512]{1,0:T(8,128)(2,1)S(1)} %collective-permute-done.1), channel_id=1, source_target_pairs={{0,24},{8,0},{16,8},{24,16},{1,25},{9,1},{17,9},{25,17},{2,26},{10... | collective-permute-start | bytes 1572872 | tf_op jit(solution)/shard_map/ppermute | solution.py:12
  63.4 4.0 %copy-start.2 = (s32[80,4]{0,1:T(4,128)S(1)}, s32[80,4]{0,1:T(4,128)}, u32[]{:S(2)}) copy-start(s32[80,4]{0,1:T(4,128)} %param.8) | copy-start | bytes 3844
  63.4 4.2 %copy-start.3 = (s32[10]{0:T(128)S(1)}, s32[10]{0:T(128)}, u32[]{:S(2)}) copy-start(s32[10]{0:T(128)} %param.9) | copy-start | bytes 124
  67.3 106.1 %reduce-scatter.2.cloned.1.call-start = ((), (), s32[]{:S(2)}) async-start(), calls=%async_computation.2 | async-start | bytes 3276800 | tf_op jit(solution)/shard_map/reduce_scatter | solution.py:49
Sparse Core Ops, SparseCore 0:
  67.4 38.6 all-gather.1
  121.1 52.2 reduce-scatter.1
